TPU v7x, 256 devices: a whole 4x4x8 slice. The times are simulated.
256 devices in a mesh: front: 4 (over y), pivot: 8 (over x, core), rows: 8 (over z).
Axes of the slice: x: 4, y: 4, z: 8, core: 2. Of those that a mesh axis runs over, the one named last changes fastest.
Arguments:
- factor: float32 [4, 8, 1024, 8192], P('front', 'pivot', 'rows'), may hold values from -0.0625 to 0.0625
- inv_diag: float32 [4, 8, 1024, 1024], P('front', 'pivot', 'rows'), may hold values from -0.1875 to 0.1875
- boundary: float32 [4, 8192, 8192], P('front', ('pivot', 'rows')), may hold values from -0.0625 to 0.0625
- rhs: float32 [4, 240, 8192], P('front', None, ('pivot', 'rows')), may hold values from -6 to 6
- boundary_rhs: float32 [4, 240, 8192], P('front', None, ('pivot', 'rows')), may hold values from -6 to 6
- owner: int32 [4, 8192, 1], P('front', ('pivot', 'rows')), may hold values from 0 to 63; in each aligned block of 128 rows (0 to 127, 128 to 255, ..., all dimensions but the last counted through in order) at most 4 rows name the same one
- slot: int32 [4, 8192], P('front', ('pivot', 'rows')), may hold values from 0 to 255
- parent_in: float32 [240, 16384], P(None, ('pivot', 'rows')), may hold values from -6 to 6
Outputs:
- solution: float32 [4, 240, 8192], P('front', None, ('pivot', 'rows'))
- parent_rhs: float32 [240, 16384], P(None, ('pivot', 'rows'))
Inputs may be any that keep to these rules, and one draw needn't show every extreme that they name: Within the 128 boundary rows of one device no owner is named more than 4 times, and in every draw some device's rows name some owner exactly 4 times.
All inputs are finite; a program needn't handle non-finite values.
Results may differ from a plain program's by a relative error of at most 0.0001.
Values sent between devices are 32-bit elements; how exact they have to be, the bound alone decides.
A program may use at most 64 MiB of HBM per device.

v0:
```python
import jax
import jax.numpy as jnp
from jax import lax
from jax.sharding import PartitionSpec as P

highest = lax.Precision.HIGHEST


def shards(factor, inv_diag, boundary, rhs, boundary_rhs, owner, slot, parent_in):
    factor_rows = factor[0, 0]
    inv_rows = inv_diag[0, 0]
    bound_rows = boundary[0]
    local_rhs = rhs[0]
    local_brhs = boundary_rhs[0]
    block_count = lax.axis_size("pivot")
    row_count = lax.axis_size("rows")
    block_span = inv_rows.shape[1]
    slice_rows = factor_rows.shape[0]
    sources = local_rhs.shape[0]
    own_block = lax.axis_index("pivot")
    own_row = lax.axis_index("rows")
    contract = (((1,), (1,)), ((), ()))

    def solve_section(section_idx, carry):
        running, boundary_sum, own_solved = carry
        residual = local_rhs - running
        partial_value = jnp.dot(
            residual, inv_rows, precision=highest, preferred_element_type=jnp.float32
        )
        masked = jnp.where(own_block == section_idx, partial_value, 0.0)
        solved = lax.psum(masked, ("pivot", "rows"))
        pivot_tile = lax.dynamic_slice_in_dim(factor_rows, section_idx * block_span, block_span, 1)
        update_term = lax.dot_general(
            solved, pivot_tile, contract, precision=highest, preferred_element_type=jnp.float32
        )
        running = running + jnp.where(section_idx < own_block, update_term, 0.0)
        bound_tile = lax.dynamic_slice_in_dim(bound_rows, section_idx * block_span, block_span, 1)
        boundary_sum = boundary_sum + lax.dot_general(
            solved, bound_tile, contract, precision=highest, preferred_element_type=jnp.float32
        )
        own_piece = lax.dynamic_slice_in_dim(solved, own_row * slice_rows, slice_rows, 1)
        own_solved = jnp.where(own_block == section_idx, own_piece, own_solved)
        return (running, boundary_sum, own_solved)

    start = (
        jnp.zeros((sources, slice_rows), jnp.float32),
        jnp.zeros((sources, bound_rows.shape[0]), jnp.float32),
        jnp.zeros((sources, slice_rows), jnp.float32),
    )
    running, boundary_sum, own_solved = lax.fori_loop(0, block_count, solve_section, start)
    update = local_brhs - boundary_sum
    out_rows = update.T
    owners = owner[0, :, 0]
    slot_ids = slot[0]
    owner_count = block_count * row_count
    capacity = max(2, 2 * out_rows.shape[0] // owner_count)
    onehot = (owners[:, None] == jnp.arange(owner_count, dtype=jnp.int32)[None, :]).astype(
        jnp.int32
    )
    before = jnp.cumsum(onehot, axis=0) - onehot
    position = jnp.sum(before * onehot, axis=1)
    dest_slot = owners * capacity + position
    select = dest_slot[None, :] == jnp.arange(owner_count * capacity, dtype=jnp.int32)[:, None]
    send_rows = jnp.dot(
        select.astype(jnp.float32), out_rows, precision=highest, preferred_element_type=jnp.float32
    )
    send_slot = jnp.max(jnp.where(select, slot_ids[None, :], -1), axis=1)
    got_rows, got_slots = (
        lax.all_to_all(
            send_rows.reshape(owner_count, capacity, sources),
            ("pivot", "rows"),
            split_axis=0,
            concat_axis=0,
            tiled=True,
        ),
        lax.all_to_all(
            send_slot.reshape(owner_count, capacity),
            ("pivot", "rows"),
            split_axis=0,
            concat_axis=0,
            tiled=True,
        ),
    )
    got_rows = got_rows.reshape(owner_count * capacity, sources)
    got_slots = got_slots.reshape(owner_count * capacity)
    parent_rows = parent_in.shape[1]
    slot_hits = (got_slots[:, None] == jnp.arange(parent_rows, dtype=jnp.int32)[None, :]).astype(
        jnp.float32
    )
    local_part = jnp.einsum(
        "ks,ko->so", got_rows, slot_hits, precision=highest, preferred_element_type=jnp.float32
    )
    sibling_total = lax.psum(local_part, "front")
    parent = parent_in + sibling_total
    return (own_solved[None], parent)


def solution(mesh):
    placed = (
        P("front", "pivot", "rows", None),
        P("front", "pivot", "rows", None),
        P("front", ("pivot", "rows"), None),
        P("front", None, ("pivot", "rows")),
        P("front", None, ("pivot", "rows")),
        P("front", ("pivot", "rows"), None),
        P("front", ("pivot", "rows")),
        P(None, ("pivot", "rows")),
    )
    return jax.shard_map(
        shards,
        mesh=mesh,
        in_specs=placed,
        out_specs=(P("front", None, ("pivot", "rows")), P(None, ("pivot", "rows"))),
        check_vma=False,
    )
```

profile of v0, /device:TPU:1, one launch (start us, length us, event | category | flops | bytes accessed | tf_op | source)
XLA Modules:
  0.0 1666.5 jit_solution(10472206007967670768)
XLA Ops:
  8.0 0.7 fusion.14
  8.7 0.2 reduce_window_sum.11
  8.9 0.8 select_reduce_fusion.1
  9.7 0.7 multiply_add_fusion
  10.4 0.8 select_reduce_fusion
  11.2 0.7 all_to_all.10
  11.9 13.0 all-to-all-start.1
  25.0 1566.7 %while.20 = (s32[]{:T(128)}, f32[240,128]{1,0:T(8,128)S(1)}, f32[240,128]{1,0:T(8,128)S(1)}, f32[240,128]{1,0:T(8,128)S(1)}, s32[]{:T(128)}, /*index=5*/f32[240,...) while((s32[]{:T(128)}, f32[240,128]{1,0:T(8,128)S(1)}, ...), condition=%wide.region_2.3_spmd.clone, body=%wide.region_0.2_spmd.clone.sunk | while | flops 1133230080 | bytes 11526409 | solution.py:50
  25.0 0.0 all-reduce.5.cloned.1.call-start
  25.0 3.1 convolution_select_fusion.3
  28.2 187.5 %all-reduce.5.cloned.1.call-done = f32[240,1024]{1,0:T(8,128)} async-done(((f32[240,1024]{1,0:T(8,128)}), f32[240,1024]{1,0:T(8,128)}) %all-reduce.5.cloned.1.call-update) | async-done | bytes 983056 | tf_op jit(solution)/shard_map/while/body/eval_jaxpr/psum | solution.py:31
  215.7 2.3 convolution_add_fusion.2
  218.0 2.3 fusion.32
  220.3 0.9 select_select_fusion.2
  221.3 3.0 convolution_select_fusion.3
  224.4 187.0 %all-reduce.5.cloned.1.call-done = f32[240,1024]{1,0:T(8,128)} async-done(((f32[240,1024]{1,0:T(8,128)}), f32[240,1024]{1,0:T(8,128)}) %all-reduce.5.cloned.1.call-update) | async-done | bytes 983056 | tf_op jit(solution)/shard_map/while/body/eval_jaxpr/psum | solution.py:31
  411.4 2.3 convolution_add_fusion.2
  413.7 2.3 fusion.32
  416.1 0.9 select_select_fusion.2
  417.1 3.0 convolution_select_fusion.3
  420.1 187.0 %all-reduce.5.cloned.1.call-done = f32[240,1024]{1,0:T(8,128)} async-done(((f32[240,1024]{1,0:T(8,128)}), f32[240,1024]{1,0:T(8,128)}) %all-reduce.5.cloned.1.call-update) | async-done | bytes 983056 | tf_op jit(solution)/shard_map/while/body/eval_jaxpr/psum | solution.py:31
  607.1 2.3 convolution_add_fusion.2
  609.5 2.3 fusion.32
  611.8 0.9 select_select_fusion.2
  612.8 0.0 all-reduce.5.cloned.1.call-start
  612.8 3.0 convolution_select_fusion.3
  615.9 186.7 %all-reduce.5.cloned.1.call-done = f32[240,1024]{1,0:T(8,128)} async-done(((f32[240,1024]{1,0:T(8,128)}), f32[240,1024]{1,0:T(8,128)}) %all-reduce.5.cloned.1.call-update) | async-done | bytes 983056 | tf_op jit(solution)/shard_map/while/body/eval_jaxpr/psum | solution.py:31
  802.6 2.3 convolution_add_fusion.2
  804.9 2.3 fusion.32
  807.2 0.9 select_select_fusion.2
  808.2 0.0 all-reduce.5.cloned.1.call-start
  808.2 3.0 convolution_select_fusion.3
  811.3 186.7 %all-reduce.5.cloned.1.call-done = f32[240,1024]{1,0:T(8,128)} async-done(((f32[240,1024]{1,0:T(8,128)}), f32[240,1024]{1,0:T(8,128)}) %all-reduce.5.cloned.1.call-update) | async-done | bytes 983056 | tf_op jit(solution)/shard_map/while/body/eval_jaxpr/psum | solution.py:31
  998.0 2.3 convolution_add_fusion.2
  1000.3 2.3 fusion.32
  1002.6 0.9 select_select_fusion.2
  1003.6 0.0 all-reduce.5.cloned.1.call-start
  1003.6 3.0 convolution_select_fusion.3
  1006.7 187.4 %all-reduce.5.cloned.1.call-done = f32[240,1024]{1,0:T(8,128)} async-done(((f32[240,1024]{1,0:T(8,128)}), f32[240,1024]{1,0:T(8,128)}) %all-reduce.5.cloned.1.call-update) | async-done | bytes 983056 | tf_op jit(solution)/shard_map/while/body/eval_jaxpr/psum | solution.py:31
  1194.1 2.3 convolution_add_fusion.2
  1196.5 2.3 fusion.32
  1198.8 0.9 select_select_fusion.2
  1199.8 3.0 convolution_select_fusion.3
  1202.9 187.4 %all-reduce.5.cloned.1.call-done = f32[240,1024]{1,0:T(8,128)} async-done(((f32[240,1024]{1,0:T(8,128)}), f32[240,1024]{1,0:T(8,128)}) %all-reduce.5.cloned.1.call-update) | async-done | bytes 983056 | tf_op jit(solution)/shard_map/while/body/eval_jaxpr/psum | solution.py:31
  1390.3 2.3 convolution_add_fusion.2
  1392.6 2.3 fusion.32
  1394.9 0.9 select_select_fusion.2
  1396.0 3.0 convolution_select_fusion.3
  1399.0 187.0 %all-reduce.5.cloned.1.call-done = f32[240,1024]{1,0:T(8,128)} async-done(((f32[240,1024]{1,0:T(8,128)}), f32[240,1024]{1,0:T(8,128)}) %all-reduce.5.cloned.1.call-update) | async-done | bytes 983056 | tf_op jit(solution)/shard_map/while/body/eval_jaxpr/psum | solution.py:31
  1586.1 2.3 convolution_add_fusion.2
  1588.4 2.3 fusion.32
  1590.7 0.9 select_select_fusion.2
  1591.7 0.3 fusion.12
  1592.0 0.8 reshape.25
  1592.8 9.8 all-to-all-start
  1602.6 0.0 all-reduce.3.cloned.1.call-start
  1602.6 0.5 broadcast.42
  1603.1 0.7 reduce.3
  1603.9 0.1 eq.57
  1604.0 10.6 all-to-all-done
  1614.6 0.1 reshape.26
  1614.7 1.1 fusion.10
  1615.9 41.5 %all-reduce.3.cloned.1.call-done = f32[240,256]{1,0:T(8,128)} async-done(((f32[240,256]{1,0:T(8,128)}), f32[240,256]{1,0:T(8,128)}) %all-reduce.3.cloned.1.call-update) | async-done | bytes 245776 | tf_op jit(solution)/shard_map/psum | solution.py:93
  1657.4 1.7 add.72
  (23 shorter events, 0.3 us)
Async XLA Ops:
  11.9 1580.9 %all-to-all-start.1 = ((s32[64,1,4]{2,1,0:T(1,128)}), s32[64,1,4]{2,1,0:T(1,128)S(1)}, u32[]{:S(2)}, u32[]{:S(2)}) async-start(s32[64,1,4]{2,1,0:T(1,128)} %bitcast.8), calls=%async_computation.1 | async-start | bytes 65536 | tf_op jit(solution)/shard_map/all_to_all | solution.py:76
  24.9 1566.7 %copy-start.2 = (f32[1,240,128]{2,1,0:T(8,128)S(1)}, f32[1,240,128]{2,1,0:T(8,128)}, u32[]{:S(2)}) copy-start(f32[1,240,128]{2,1,0:T(8,128)} %param.14) | copy-start | bytes 368644
  24.9 1632.5 %copy-start.1 = (f32[240,256]{1,0:T(8,128)S(1)}, f32[240,256]{1,0:T(8,128)}, u32[]{:S(2)}) copy-start(f32[240,256]{1,0:T(8,128)} %param.17) | copy-start | bytes 737284
  25.0 190.7 %all-reduce.5.cloned.1.call-start = ((), (), s32[]{:S(2)}) async-start(), calls=%async_computation.3 | async-start | bytes 1966080 | tf_op jit(solution)/shard_map/while/body/eval_jaxpr/psum | solution.py:31
  221.3 190.1 %all-reduce.5.cloned.1.call-start = ((), (), s32[]{:S(2)}) async-start(), calls=%async_computation.3 | async-start | bytes 1966080 | tf_op jit(solution)/shard_map/while/body/eval_jaxpr/psum | solution.py:31
  417.0 190.1 %all-reduce.5.cloned.1.call-start = ((), (), s32[]{:S(2)}) async-start(), calls=%async_computation.3 | async-start | bytes 1966080 | tf_op jit(solution)/shard_map/while/body/eval_jaxpr/psum | solution.py:31
  612.8 189.8 %all-reduce.5.cloned.1.call-start = ((), (), s32[]{:S(2)}) async-start(), calls=%async_computation.3 | async-start | bytes 1966080 | tf_op jit(solution)/shard_map/while/body/eval_jaxpr/psum | solution.py:31
  808.2 189.8 %all-reduce.5.cloned.1.call-start = ((), (), s32[]{:S(2)}) async-start(), calls=%async_computation.3 | async-start | bytes 1966080 | tf_op jit(solution)/shard_map/while/body/eval_jaxpr/psum | solution.py:31
  1003.6 190.5 %all-reduce.5.cloned.1.call-start = ((), (), s32[]{:S(2)}) async-start(), calls=%async_computation.3 | async-start | bytes 1966080 | tf_op jit(solution)/shard_map/while/body/eval_jaxpr/psum | solution.py:31
  1199.7 190.6 %all-reduce.5.cloned.1.call-start = ((), (), s32[]{:S(2)}) async-start(), calls=%async_computation.3 | async-start | bytes 1966080 | tf_op jit(solution)/shard_map/while/body/eval_jaxpr/psum | solution.py:31
  1395.9 190.1 %all-reduce.5.cloned.1.call-start = ((), (), s32[]{:S(2)}) async-start(), calls=%async_computation.3 | async-start | bytes 1966080 | tf_op jit(solution)/shard_map/while/body/eval_jaxpr/psum | solution.py:31
  1591.7 67.5 %copy-start = (f32[240,128]{1,0:T(8,128)}, f32[240,128]{1,0:T(8,128)S(1)}, u32[]{:S(2)}) copy-start(f32[240,128]{1,0:T(8,128)S(1)} %get-tuple-element.239) | copy-start | bytes 368644
  1592.8 21.8 %all-to-all-start = ((f32[64,4,240]{2,1,0:T(4,128)}), f32[64,4,240]{2,1,0:T(4,128)S(1)}, u32[]{:S(2)}, u32[]{:S(2)}) async-start(f32[64,4,240]{2,1,0:T(4,128)} %reshape.25), calls=%async_computation | async-start | bytes 524288 | tf_op jit(solution)/shard_map/all_to_all | solution.py:69
  1602.6 54.8 %all-reduce.3.cloned.1.call-start = ((), (), s32[]{:S(2)}) async-start(), calls=%async_computation.2 | async-start | bytes 491520 | tf_op jit(solution)/shard_map/psum | solution.py:93
Sparse Core Ops, SparseCore 0:
  29.2 186.4 all-reduce.4
  225.5 185.8 all-reduce.4
  421.2 185.8 all-reduce.4
  616.6 185.8 all-reduce.4
  812.0 185.8 all-reduce.4
  1007.5 186.6 all-reduce.4
  1203.9 186.3 all-reduce.4
  1400.1 185.9 all-reduce.4
Sparse Core Ops, SparseCore 1:
  1615.9 41.4 all-reduce.2
where the time goes:
time: 1670 us
  waiting for transfers between devices  1550 us (93%)
  matrix products  62.8 us (4%)
  starting transfers between devices  23.2 us (1%)
    psum x8, waiting for transfers between devices, solve_section(): solved = lax.psum(masked, ('pivot', 'rows'))  1500 us
    psum x1, waiting for transfers between devices, shards(): sibling_total = lax.psum(local_part, 'front')  41.5 us
  transfers between devices with their start and end apart: 11, of which 10 were waited for; matrix products, arithmetic and copies ran while one was open for 4% of the time, Pallas kernels for 0%

commit v1 on v0

v1 whole, which is shorter than its diff:
```python
import functools

import jax
import jax.numpy as jnp
from jax import lax
from jax.experimental import pallas as pl
from jax.experimental.pallas import tpu as pltpu
from jax.sharding import PartitionSpec as P

MESH = pl.DeviceIdType.MESH
F32, BF16 = jnp.float32, jnp.bfloat16
NT = (((1,), (1,)), ((), ()))
NN = (((1,), (0,)), ((), ()))
NP, NR, W = 8, 8, 128
CAP = 4


def halves(x):
    hi = x.astype(BF16)
    return hi, (x - hi.astype(F32)).astype(BF16)


def mul(a, b, dims):
    return lax.dot_general(a, b, dims, preferred_element_type=F32)


def arrived(ref, sem):
    pltpu.make_async_copy(ref, ref, sem).wait()


def kernel(
    chunks, fronts, fac, bnd, inv, rhs, brhs, own, slot, par, out_sol, out_par,
    stage, wh, wl, inv_cols, inv_hl, gath, solved, mine, acc, tosend, got, part, quarters, summed,
    load_sem, inv_s, inv_r, g1_s, g1_r, st_s, ag_s, ag_r, fw_s, fw_r, own_s, own_r,
    rs_s, rs_r, fa_s, fa_r,
):
    f, p, z = lax.axis_index("front"), lax.axis_index("pivot"), lax.axis_index("rows")
    me = p * NR + z
    core = lax.rem(p, 2)
    col = p // 2
    span = NR * W
    peers = NP * NR

    def at_z(d):
        return lax.rem(z + d + NR, NR)

    def lanes(i):
        return pl.ds(pl.multiple_of(i * W, W), W)

    def remote(src, dst, ssem, rsem, dev):
        return pltpu.make_async_remote_copy(
            src_ref=src, dst_ref=dst, send_sem=ssem, recv_sem=rsem, device_id=dev, device_id_type=MESH
        )

    load_f = pltpu.make_async_copy(fac, stage.at[pl.ds(0, W)], load_sem.at[0])
    load_b = pltpu.make_async_copy(bnd, stage.at[pl.ds(W, W)], load_sem.at[1])
    load_i = pltpu.make_async_copy(inv.at[:, lanes(z)], inv_cols.at[lanes(z), :], load_sem.at[2])
    load_f.start()
    load_b.start()
    load_i.start()

    barrier = pltpu.get_barrier_semaphore()

    @pl.loop(1, peers)
    def _(i):
        t = lax.rem(me + i, peers)
        pl.semaphore_signal(barrier, inc=1, device_id=(f, t // NR, lax.rem(t, NR)), device_id_type=MESH)

    for i in range(1, fronts):
        pl.semaphore_signal(barrier, inc=1, device_id=(lax.rem(f + i, fronts), p, z), device_id_type=MESH)
    pl.semaphore_wait(barrier, peers + fronts - 2)

    def spread(buf, rows, ssem, rsem):
        for j, d in ((2, 2), (3, -2), (0, 1), (1, -1)):
            piece = buf.at[rows, lanes(z)]
            remote(piece, piece, ssem.at[j], rsem.at[j], (f, p, at_z(d))).start()

    def part_of(rows, second):
        n = rows.size // 2
        return pl.ds(rows.start + (n if second else 0), n)

    def relay(buf, rows, ssem, rsem):
        for j, d in ((2, 1), (3, -1)):
            src = lanes(at_z(-2 * d))
            piece = buf.at[rows, src]
            arrived(piece, rsem.at[j])
            remote(piece, piece, ssem.at[j + 2], rsem.at[j + 2], (f, p, at_z(d))).start()
            some = buf.at[part_of(rows, d < 0), src]
            remote(some, some, ssem.at[j + 4], rsem.at[j + 4], (f, p, at_z(2 * d))).start()

    def finish(buf, rows, rsem):
        for j, d in ((0, -1), (1, 1), (4, -3), (5, 3)):
            arrived(buf.at[rows, lanes(at_z(d))], rsem.at[j])
        far = lanes(at_z(4))
        arrived(buf.at[part_of(rows, False), far], rsem.at[6])
        arrived(buf.at[part_of(rows, True), far], rsem.at[7])

    def sent(buf, rows, ssem):
        for j in range(6):
            arrived(buf.at[rows, lanes(z)], ssem.at[j])
        for j in (6, 7):
            arrived(buf.at[part_of(rows, False), lanes(z)], ssem.at[j])

    def start_block(c, rows):
        base = rhs[rows, :] - acc[rows, pl.ds(0, W)]
        gath[rows, lanes(z)] = base
        spread(gath, rows, g1_s.at[c], g1_r.at[c])

    acc[...] = jnp.zeros_like(acc)

    @pl.when(p == 0)
    def _():
        for c, rows in enumerate(chunks):
            start_block(c, rows)

    for d in range(1, NR):
        remote(
            inv.at[:, lanes(at_z(d))], inv_cols.at[lanes(z), :], inv_s.at[d - 1], inv_r.at[d - 1], (f, p, at_z(d))
        ).start()

    load_f.wait()
    load_b.wait()

    @pl.loop(0, NP)
    def _(k):
        cols = pl.ds(pl.multiple_of(k * span, span), span)
        hi, lo = halves(stage[:, cols])
        wh[:, cols] = hi
        wl[:, cols] = lo

    load_i.wait()
    for d in range(1, NR):
        arrived(inv_cols.at[lanes(at_z(-d)), :], inv_r.at[d - 1])
    hi, lo = halves(inv_cols[...])
    inv_hl[:, pl.ds(0, W)] = hi
    inv_hl[:, pl.ds(W, W)] = lo

    @pl.loop(0, NP)
    def _(k):
        lead = 1 - lax.rem(k, 2)
        block = solved.at[k]

        @pl.when(p == k)
        def _():
            for c, rows in enumerate(chunks):
                relay(gath, rows, g1_s.at[c], g1_r.at[c])
            for c, rows in enumerate(chunks):
                finish(gath, rows, g1_r.at[c])
                hi, lo = halves(gath[rows, :])
                both = mul(hi, inv_hl[...], NN)
                mine[rows, :] = both[:, :W] + both[:, W:] + mul(lo, inv_hl[:, pl.ds(0, W)], NN)
                for i in range(NP // 2):
                    to = lax.rem(col + i + (k % 2), NP // 2)
                    remote(
                        mine.at[rows, :], block.at[rows, lanes(z)], st_s.at[c, i], ag_r.at[k, c, 8],
                        (f, to * 2 + lead, z),
                    ).start()

        @pl.when(core == lead)
        def _():
            for c, rows in enumerate(chunks):
                arrived(block.at[rows, lanes(z)], ag_r.at[k, c, 8])
                spread(block, rows, ag_s.at[c], ag_r.at[k, c])
            for c, rows in enumerate(chunks):
                relay(block, rows, ag_s.at[c], ag_r.at[k, c])

        for c, rows in enumerate(chunks):

            @pl.when(core == lead)
            def _():
                finish(block, rows, ag_r.at[k, c])
                remote(
                    block.at[rows, :], block.at[rows, :], fw_s.at[c], fw_r.at[k, c],
                    (f, col * 2 + 1 - lead, z),
                ).start()

            @pl.when(core != lead)
            def _():
                arrived(block.at[rows, :], fw_r.at[k, c])

            cols = pl.ds(pl.multiple_of(k * span, span), span)
            hi, lo = halves(block[rows, :])
            acc[rows, :] += mul(hi, wh[:, cols], NT) + mul(lo, wh[:, cols], NT) + mul(hi, wl[:, cols], NT)

            @pl.when(p == k + 1)
            def _():
                start_block(c, rows)

        @pl.when((core != lead) & (k > 0))
        def _():
            for c, rows in enumerate(chunks):
                sent(block, rows, ag_s.at[c])
                arrived(block.at[rows, :], fw_s.at[c])

    half = mine.shape[0] // 2
    owner_col = jnp.broadcast_to(own[...], (W, W)).astype(F32)
    owner_row = owner_col.T
    first = lax.broadcasted_iota(jnp.int32, (W, W), 0)
    second = lax.broadcasted_iota(jnp.int32, (W, W), 1)
    earlier = jnp.where((owner_col == owner_row) & (first < second), 1.0, 0.0)
    position = jnp.sum(earlier, axis=0, keepdims=True)
    tile = owner_row[0:1, :] * (2 * CAP) + position
    row_id = lax.broadcasted_iota(jnp.int32, (peers * 2 * CAP, W), 0).astype(F32)
    pick = jnp.concatenate(
        [jnp.where(row_id == tile, 1.0, 0.0), jnp.where(row_id == tile + CAP, 1.0, 0.0)], axis=1
    ).astype(BF16)
    update = brhs[...] - acc[:, pl.ds(W, W)]
    tail = jnp.where(
        lax.broadcasted_iota(jnp.int32, (W - half, W), 0) == 0,
        jnp.broadcast_to(slot[...], (W - half, W)).astype(F32),
        0.0,
    )
    ext = jnp.concatenate(
        [
            jnp.concatenate([update[:half], tail], axis=0),
            jnp.concatenate([update[half:], tail], axis=0),
        ],
        axis=1,
    )
    hi, lo = halves(ext)
    tosend[...] = mul(pick, hi, NT) + mul(pick, lo, NT)

    def tiles(i):
        return pl.ds(pl.multiple_of(i * 2 * CAP, 2 * CAP), 2 * CAP)

    @pl.loop(1, peers)
    def _(i):
        t = lax.rem(me + i, peers)
        remote(
            tosend.at[tiles(t), :], got.at[tiles(me), :], own_s.at[i], own_r.at[i],
            (f, t // NR, lax.rem(t, NR)),
        ).start()

    got[tiles(me), :] = tosend[tiles(me), :]

    @pl.loop(1, peers)
    def _(i):
        t = lax.rem(me + peers - i, peers)
        arrived(got.at[tiles(t), :], own_r.at[i])

    flat = got[...].T
    slots = flat[half:half + 1, :]
    hits = jnp.where(
        slots == lax.broadcasted_iota(jnp.int32, (par.shape[1], peers * 2 * CAP), 0).astype(F32), 1.0, 0.0
    ).astype(BF16)
    which = lax.rem(lax.broadcasted_iota(jnp.int32, (W, peers * 2 * CAP), 1) // CAP, 2)
    both = jnp.concatenate([jnp.where(which == 0, flat, 0.0), jnp.where(which == 1, flat, 0.0)], axis=0)
    hi, lo = halves(both)
    part[...] = mul(hi, hits, NT) + mul(lo, hits, NT)

    band = 2 * W // fronts

    def bands(i):
        return pl.ds(pl.multiple_of(i * band, band), band)

    for i in range(1, fronts):
        t = lax.rem(f + i, fronts)
        remote(part.at[bands(t), :], quarters.at[i - 1], rs_s.at[i - 1], rs_r.at[i - 1], (t, p, z)).start()
    for i in range(1, fronts):
        arrived(quarters.at[i - 1], rs_r.at[i - 1])
    total = part[bands(f), :]
    for i in range(1, fronts):
        total = total + quarters[i - 1]
    for i in range(1, fronts):
        arrived(quarters.at[i - 1], rs_s.at[i - 1])
    summed[bands(f), :] = total
    for i in range(1, fronts):
        t = lax.rem(f + i, fronts)
        remote(summed.at[bands(f), :], summed.at[bands(f), :], fa_s.at[i - 1], fa_r.at[i - 1], (t, p, z)).start()
    for i in range(1, fronts):
        arrived(summed.at[bands(lax.rem(f + fronts - i, fronts)), :], fa_r.at[i - 1])
    out_par[0:half, :] = par[0:half, :] + summed[0:half, :]
    out_par[half:2 * half, :] = par[half:2 * half, :] + summed[W:W + half, :]
    out_sol[...] = mine[...]

    for d in range(1, NR):
        arrived(inv_cols.at[lanes(z), :], inv_s.at[d - 1])
    for c, rows in enumerate(chunks):
        sent(gath, rows, g1_s.at[c])
        for i in range(NP // 2):
            arrived(mine.at[rows, :], st_s.at[c, i])

    @pl.when(core == 0)
    def _():
        for c, rows in enumerate(chunks):
            sent(solved.at[0], rows, ag_s.at[c])
            arrived(solved.at[0].at[rows, :], fw_s.at[c])

    @pl.loop(1, peers)
    def _(i):
        arrived(tosend.at[tiles(0), :], own_s.at[i])

    for i in range(1, fronts):
        arrived(part.at[bands(f), :], fa_s.at[i - 1])


def shards(factor, inv_diag, boundary, rhs, boundary_rhs, owner, slot, parent_in):
    fronts = lax.axis_size("front")
    sources = rhs.shape[1]
    depth = factor.shape[3]
    span = NR * W
    rows = parent_in.shape[1]
    first = (sources // 2 + 15) // 16 * 16
    chunks = (pl.ds(0, first), pl.ds(first, sources - first))
    ns = len(chunks)
    any_spec, vmem = pl.BlockSpec(memory_space=pl.ANY), pl.BlockSpec(memory_space=pltpu.VMEM)
    dma = pltpu.SemaphoreType.DMA
    return pl.pallas_call(
        functools.partial(kernel, chunks, fronts),
        out_shape=(
            jax.ShapeDtypeStruct((sources, W), F32),
            jax.ShapeDtypeStruct((sources, rows), F32),
        ),
        in_specs=[any_spec] * 3 + [vmem] * 5,
        out_specs=(vmem, vmem),
        scratch_shapes=[
            pltpu.VMEM((2 * W, depth), F32),
            pltpu.VMEM((2 * W, depth), BF16),
            pltpu.VMEM((2 * W, depth), BF16),
            pltpu.VMEM((span, W), F32),
            pltpu.VMEM((span, 2 * W), BF16),
            pltpu.VMEM((sources, span), F32),
            pltpu.VMEM((NP, sources, span), F32),
            pltpu.VMEM((sources, W), F32),
            pltpu.VMEM((sources, 2 * W), F32),
            pltpu.VMEM((NP * NR * 2 * CAP, W), F32),
            pltpu.VMEM((NP * NR * 2 * CAP, W), F32),
            pltpu.VMEM((2 * W, rows), F32),
            pltpu.VMEM((max(1, fronts - 1), 2 * W // fronts, rows), F32),
            pltpu.VMEM((2 * W, rows), F32),
            dma((3,)),
            dma((NR - 1,)),
            dma((NR - 1,)),
            dma((ns, 8)),
            dma((ns, 8)),
            dma((ns, NP // 2)),
            dma((ns, 8)),
            dma((NP, ns, 9)),
            dma((ns,)),
            dma((NP, ns)),
            dma((NP * NR,)),
            dma((NP * NR,)),
            dma((fronts,)),
            dma((fronts,)),
            dma((fronts,)),
            dma((fronts,)),
        ],
        compiler_params=pltpu.CompilerParams(collective_id=0, has_side_effects=True, vmem_limit_bytes=60 << 20),
    )(factor[0, 0], boundary[0], inv_diag[0, 0], rhs[0], boundary_rhs[0], owner[0], slot, parent_in)


def body(*args):
    solved, parent = shards(*args)
    return solved[None], parent


def solution(mesh):
    placed = (
        P("front", "pivot", "rows", None),
        P("front", "pivot", "rows", None),
        P("front", ("pivot", "rows"), None),
        P("front", None, ("pivot", "rows")),
        P("front", None, ("pivot", "rows")),
        P("front", ("pivot", "rows"), None),
        P("front", ("pivot", "rows")),
        P(None, ("pivot", "rows")),
    )
    return jax.shard_map(
        body,
        mesh=mesh,
        in_specs=placed,
        out_specs=(P("front", None, ("pivot", "rows")), P(None, ("pivot", "rows"))),
        check_vma=False,
    )
```

time: 1670 us -> 225 us (0.13)
  waiting for transfers between devices: 1550 us -> 0 us
  Pallas kernels: 0 us -> 220 us
  matrix products: 62.8 us -> 0 us
  starting transfers between devices: 23.2 us -> 0 us
    psum x9 -> x0, waiting for transfers between devices: 1540 us -> none  [the longest x8 1500 us: solve_section(): solved = lax.psum(masked, ('pivot', 'rows'))]
    pallas_call x0 -> x1, Pallas kernels: none -> 220 us  [shards(): pl.pallas_call(functools.partial(kernel, chunks, fronts), out_shape=(jax....]
    dot_general x26 -> x0, matrix products: 62.8 us -> none  [the longest x8 24.3 us: solve_section(): jnp.dot(residual, inv_rows, precision=highest, preferred_element_type=jnp...]
    all_to_all x2 -> x0, starting transfers between devices: 22.8 us -> none  [the longest x1 13 us: shards(): lax.all_to_all(send_slot.reshape(owner_count, capacity), ('pivot', 'rows'...]
  transfers between devices with their start and end apart: 11 -> 0, of which waited for: 10 -> 0; matrix products, arithmetic and copies ran while one was open for 4% -> 0% of each run, Pallas kernels for 0% -> 0%
where the time goes in v1:
time: 225 us
  Pallas kernels  220 us (98%)
  local copies, waits for them, and re-layouts  4.6 us (2%)
    pallas_call x1, Pallas kernels, shards(): pl.pallas_call(functools.partial(kernel, chunks, fronts), out_shape=(jax....  220 us

profile of v1, /device:TPU:1, one launch (start us, length us, event | category | flops | bytes accessed | tf_op | source)
XLA Modules:
  0.0 224.8 jit_solution(2844706833174185336)
XLA Ops:
  0.6 1.4 copy.10.own
  2.0 219.5 %shard_map.95 = (f32[240,128]{1,0:T(8,128)}, f32[240,256]{1,0:T(8,128)}) custom-call(f32[128,8192]{1,0:T(8,128)} %bitcast.7, f32[128,8192]{1,0:T(8,128)} %bitcast.8, f32[128,1024]{1,0:T(8,128)} %bitcast.9, f32[240,128]{1,0:T(8,128)} %bitcast.10, f32[240,128]{1,0:T(8,128)} %bitcast.11, s32[128,1]{1,0:T(8,128)} %copy.10.own, s32[1,128]{1,0:T(1,128)} %slot.1, ...), custom_call_target="tpu_custom_call" | custom-call | tf_op jit(solution)/shard_map/pallas_call | solution.py:308
  221.5 1.6 copy.13
  223.1 1.7 copy.14

commit v2 on v1

--- a/solution.py
+++ b/solution.py
@@ -13,6 +13,7 @@
 NN = (((1,), (0,)), ((), ()))
 NP, NR, W = 8, 8, 128
 CAP = 4
+FOLDS = {4: (-1, 1, 1), 6: (-1, 1, 3)}
 
 
 def halves(x):
@@ -30,8 +31,8 @@
 
 def kernel(
     chunks, fronts, fac, bnd, inv, rhs, brhs, own, slot, par, out_sol, out_par,
-    stage, wh, wl, inv_cols, inv_hl, gath, solved, mine, acc, tosend, got, part, quarters, summed,
-    load_sem, inv_s, inv_r, g1_s, g1_r, st_s, ag_s, ag_r, fw_s, fw_r, own_s, own_r,
+    stage, wh, wl, inv_cols, inv_hl, low, gath, based, solved, mine, acc, tosend, got, part, quarters, summed,
+    load_sem, inv_s, inv_r, low_s, low_r, g1_s, g1_r, st_s, ag_s, ag_r, fw_s, fw_r, own_s, own_r,
     rs_s, rs_r, fa_s, fa_r,
 ):
     f, p, z = lax.axis_index("front"), lax.axis_index("pivot"), lax.axis_index("rows")
@@ -40,12 +41,26 @@
     col = p // 2
     span = NR * W
     peers = NP * NR
+    folds = p < 0
+    low_send, low_relay, low_use = -2, -2, -2
+    for q, (one, two, three) in FOLDS.items():
+        folds = folds | (p == q)
+        low_send = jnp.where(p == q, one, low_send)
+        low_relay = jnp.where(p == q, two, low_relay)
+        low_use = jnp.where(p == q, three, low_use)
+
+    def role(k):
+        odd = lax.rem(k, 2)
+        return 1 - odd, (odd == 0) & (col == k // 2)
 
     def at_z(d):
         return lax.rem(z + d + NR, NR)
 
     def lanes(i):
         return pl.ds(pl.multiple_of(i * W, W), W)
+
+    def wide(k):
+        return pl.ds(pl.multiple_of(k * span, span), span)
 
     def remote(src, dst, ssem, rsem, dev):
         return pltpu.make_async_remote_copy(
@@ -70,41 +85,98 @@
         pl.semaphore_signal(barrier, inc=1, device_id=(lax.rem(f + i, fronts), p, z), device_id_type=MESH)
     pl.semaphore_wait(barrier, peers + fronts - 2)
 
-    def spread(buf, rows, ssem, rsem):
-        for j, d in ((2, 2), (3, -2), (0, 1), (1, -1)):
-            piece = buf.at[rows, lanes(z)]
-            remote(piece, piece, ssem.at[j], rsem.at[j], (f, p, at_z(d))).start()
-
-    def part_of(rows, second):
-        n = rows.size // 2
-        return pl.ds(rows.start + (n if second else 0), n)
-
-    def relay(buf, rows, ssem, rsem):
+    def by_lanes(buf, rows):
+        def piece(i, half=None):
+            if half is None:
+                return buf.at[rows, lanes(i)]
+            return buf.at[pl.ds(rows.start + half * (rows.size // 2), rows.size // 2), lanes(i)]
+
+        return piece
+
+    def by_rows(buf):
+        def piece(i, half=None):
+            if half is None:
+                return buf.at[lanes(i), :]
+            return buf.at[pl.ds(pl.multiple_of(i * W + half * (W // 2), W // 2), W // 2), :]
+
+        return piece
+
+    near = ((2, 2), (3, -2), (0, 1), (1, -1))
+
+    def spread(piece, src, ssem, rsem):
+        for j, d in near:
+            remote(src, piece(z), ssem.at[j], rsem.at[j], (f, p, at_z(d))).start()
+
+    def relay(piece, ssem, rsem):
         for j, d in ((2, 1), (3, -1)):
-            src = lanes(at_z(-2 * d))
-            piece = buf.at[rows, src]
-            arrived(piece, rsem.at[j])
-            remote(piece, piece, ssem.at[j + 2], rsem.at[j + 2], (f, p, at_z(d))).start()
-            some = buf.at[part_of(rows, d < 0), src]
+            origin = at_z(-2 * d)
+            arrived(piece(origin), rsem.at[j])
+            remote(piece(origin), piece(origin), ssem.at[j + 2], rsem.at[j + 2], (f, p, at_z(d))).start()
+            some = piece(origin, j - 2)
             remote(some, some, ssem.at[j + 4], rsem.at[j + 4], (f, p, at_z(2 * d))).start()
 
-    def finish(buf, rows, rsem):
+    def finish(piece, rsem):
         for j, d in ((0, -1), (1, 1), (4, -3), (5, 3)):
-            arrived(buf.at[rows, lanes(at_z(d))], rsem.at[j])
-        far = lanes(at_z(4))
-        arrived(buf.at[part_of(rows, False), far], rsem.at[6])
-        arrived(buf.at[part_of(rows, True), far], rsem.at[7])
-
-    def sent(buf, rows, ssem):
-        for j in range(6):
-            arrived(buf.at[rows, lanes(z)], ssem.at[j])
-        for j in (6, 7):
-            arrived(buf.at[part_of(rows, False), lanes(z)], ssem.at[j])
+            arrived(piece(at_z(d)), rsem.at[j])
+        for h in (0, 1):
+            arrived(piece(at_z(4), h), rsem.at[6 + h])
+
+    def sent_near(piece, ssem):
+        for j in range(4):
+            arrived(piece(z), ssem.at[j])
+
+    def sent_far(piece, ssem):
+        for j in (4, 5):
+            arrived(piece(z), ssem.at[j])
+        for h in (0, 1):
+            arrived(piece(z, h), ssem.at[6 + h])
 
     def start_block(c, rows):
-        base = rhs[rows, :] - acc[rows, pl.ds(0, W)]
-        gath[rows, lanes(z)] = base
-        spread(gath, rows, g1_s.at[c], g1_r.at[c])
+        gath[rows, lanes(z)] = rhs[rows, :] - acc[rows, pl.ds(0, W)]
+        piece = by_lanes(gath, rows)
+        spread(piece, piece(z), g1_s.at[c], g1_r.at[c])
+
+    def gathered(c, rows):
+        finish(by_lanes(gath, rows), g1_r.at[c])
+        hi, lo = halves(gath[rows, :])
+        both = mul(hi, inv_hl[...], NN)
+        return both[:, :W] + both[:, W:] + mul(lo, inv_hl[:, pl.ds(0, W)], NN)
+
+    def send_solved(k, c, rows):
+        target = lax.rem(k + 1, NP)
+        odd = lax.rem(k, 2)
+        src, dst = mine.at[rows, :], solved.at[k].at[rows, lanes(z)]
+
+        def to(n, j, pivot, d):
+            remote(src, dst, st_s.at[c, n], ag_r.at[k, c, j], (f, lax.rem(pivot, NP), at_z(d))).start()
+
+        @pl.when(odd == 0)
+        def _():
+            for j, d in near:
+                to(j, j, target, d)
+
+        for i in range(NP // 2):
+            to(4 + i, 8, target + 2 * i, 0)
+
+    def send_low():
+        src = fac.at[:, wide(p - 1)]
+        spread(by_rows(low), src, low_s, low_r)
+        pltpu.make_async_copy(src, low.at[lanes(z), :], load_sem.at[3]).start()
+
+    def sent_block(k, when):
+        lead, direct = role(k)
+
+        @pl.when((core == lead) & when)
+        def _():
+            for c, rows in enumerate(chunks):
+                piece = by_lanes(solved.at[0], rows)
+
+                @pl.when(jnp.logical_not(direct))
+                def _():
+                    sent_near(piece, ag_s.at[lax.rem(k, 2), c])
+
+                sent_far(piece, ag_s.at[lax.rem(k, 2), c])
+                arrived(solved.at[0].at[rows, :], fw_s.at[lax.rem(k, 2), c])
 
     acc[...] = jnp.zeros_like(acc)
 
@@ -113,20 +185,37 @@
         for c, rows in enumerate(chunks):
             start_block(c, rows)
 
-    for d in range(1, NR):
-        remote(
-            inv.at[:, lanes(at_z(d))], inv_cols.at[lanes(z), :], inv_s.at[d - 1], inv_r.at[d - 1], (f, p, at_z(d))
-        ).start()
+    def send_inv():
+        for d in range(1, NR):
+            remote(
+                inv.at[:, lanes(at_z(d))], inv_cols.at[lanes(z), :], inv_s.at[d - 1], inv_r.at[d - 1], (f, p, at_z(d))
+            ).start()
+
+    @pl.when(core == 0)
+    def _():
+        send_inv()
+
+    @pl.when(low_send == -1)
+    def _():
+        send_low()
+
+    @pl.when(p == 0)
+    def _():
+        for c, rows in enumerate(chunks):
+            relay(by_lanes(gath, rows), g1_s.at[c], g1_r.at[c])
 
     load_f.wait()
     load_b.wait()
 
     @pl.loop(0, NP)
     def _(k):
-        cols = pl.ds(pl.multiple_of(k * span, span), span)
-        hi, lo = halves(stage[:, cols])
-        wh[:, cols] = hi
-        wl[:, cols] = lo
+        hi, lo = halves(stage[:, wide(k)])
+        wh[:, wide(k)] = hi
+        wl[:, wide(k)] = lo
+
+    @pl.when(core == 1)
+    def _():
+        send_inv()
 
     load_i.wait()
     for d in range(1, NR):
@@ -137,60 +226,100 @@
 
     @pl.loop(0, NP)
     def _(k):
-        lead = 1 - lax.rem(k, 2)
+        lead, direct = role(k)
         block = solved.at[k]
-
-        @pl.when(p == k)
-        def _():
+        par_k = lax.rem(k, 2)
+
+        @pl.when((p == k) & jnp.logical_not(folds))
+        def _():
+            @pl.when(k > 0)
+            def _():
+                for c, rows in enumerate(chunks):
+                    relay(by_lanes(gath, rows), g1_s.at[c], g1_r.at[c])
+
             for c, rows in enumerate(chunks):
-                relay(gath, rows, g1_s.at[c], g1_r.at[c])
-            for c, rows in enumerate(chunks):
-                finish(gath, rows, g1_r.at[c])
-                hi, lo = halves(gath[rows, :])
-                both = mul(hi, inv_hl[...], NN)
-                mine[rows, :] = both[:, :W] + both[:, W:] + mul(lo, inv_hl[:, pl.ds(0, W)], NN)
-                for i in range(NP // 2):
-                    to = lax.rem(col + i + (k % 2), NP // 2)
-                    remote(
-                        mine.at[rows, :], block.at[rows, lanes(z)], st_s.at[c, i], ag_r.at[k, c, 8],
-                        (f, to * 2 + lead, z),
-                    ).start()
-
-        @pl.when(core == lead)
-        def _():
-            for c, rows in enumerate(chunks):
-                arrived(block.at[rows, lanes(z)], ag_r.at[k, c, 8])
-                spread(block, rows, ag_s.at[c], ag_r.at[k, c])
-            for c, rows in enumerate(chunks):
-                relay(block, rows, ag_s.at[c], ag_r.at[k, c])
+                mine[rows, :] = gathered(c, rows)
+                send_solved(k, c, rows)
 
         for c, rows in enumerate(chunks):
+            piece = by_lanes(block, rows)
+
+            @pl.when((core == lead) & jnp.logical_not(direct))
+            def _():
+                arrived(piece(z), ag_r.at[k, c, 8])
+                spread(piece, piece(z), ag_s.at[par_k, c], ag_r.at[k, c])
+
+        for c, rows in enumerate(chunks):
 
             @pl.when(core == lead)
             def _():
-                finish(block, rows, ag_r.at[k, c])
+                relay(by_lanes(block, rows), ag_s.at[par_k, c], ag_r.at[k, c])
+
+            @pl.when((p == k + 1) & folds)
+            def _():
+                relay(by_lanes(gath, rows), g1_s.at[c], g1_r.at[c])
+
+        for c, rows in enumerate(chunks):
+
+            @pl.when((p == k + 1) & folds)
+            def _():
+                based[rows, :] = gathered(c, rows)
+
+            @pl.when(core == lead)
+            def _():
+                piece = by_lanes(block, rows)
+
+                @pl.when(direct)
+                def _():
+                    arrived(piece(z), ag_r.at[k, c, 8])
+
+                finish(piece, ag_r.at[k, c])
                 remote(
-                    block.at[rows, :], block.at[rows, :], fw_s.at[c], fw_r.at[k, c],
-                    (f, col * 2 + 1 - lead, z),
+                    block.at[rows, :], block.at[rows, :], fw_s.at[par_k, c], fw_r.at[k, c], (f, col * 2 + 1 - lead, z)
                 ).start()
 
             @pl.when(core != lead)
             def _():
                 arrived(block.at[rows, :], fw_r.at[k, c])
 
-            cols = pl.ds(pl.multiple_of(k * span, span), span)
             hi, lo = halves(block[rows, :])
-            acc[rows, :] += mul(hi, wh[:, cols], NT) + mul(lo, wh[:, cols], NT) + mul(hi, wl[:, cols], NT)
-
-            @pl.when(p == k + 1)
+            term = mul(hi, wh[:, wide(k)], NT) + mul(lo, wh[:, wide(k)], NT) + mul(hi, wl[:, wide(k)], NT)
+
+            @pl.when((p == k + 1) & folds)
+            def _():
+                mine[rows, :] = based[rows, :] - term[:, :W]
+                send_solved(k + 1, c, rows)
+
+            acc[rows, :] += term
+
+            @pl.when(jnp.where(folds, p == k + 2, p == k + 1))
             def _():
                 start_block(c, rows)
 
-        @pl.when((core != lead) & (k > 0))
-        def _():
-            for c, rows in enumerate(chunks):
-                sent(block, rows, ag_s.at[c])
-                arrived(block.at[rows, :], fw_s.at[c])
+        @pl.when(low_send == k)
+        def _():
+            send_low()
+
+        @pl.when(low_relay == k)
+        def _():
+            relay(by_rows(low), low_s, low_r)
+
+        @pl.when(low_use == k)
+        def _():
+            finish(by_rows(low), low_r)
+            pltpu.make_async_copy(low.at[lanes(z), :], low.at[lanes(z), :], load_sem.at[3]).wait()
+            ih, il = halves(inv_cols[...].T)
+
+            @pl.loop(0, span // (2 * W))
+            def _(i):
+                some = pl.ds(pl.multiple_of(i * 2 * W, 2 * W), 2 * W)
+                hi, lo = halves(low[:, some])
+                hi, lo = halves(mul(ih, hi, NN) + mul(il, hi, NN) + mul(ih, lo, NN))
+                into = pl.ds(pl.multiple_of((p - 1) * span + i * 2 * W, 2 * W), 2 * W)
+                wh[pl.ds(0, W), into] = hi
+                wl[pl.ds(0, W), into] = lo
+
+        sent_block(k - 1, k > 0)
 
     half = mine.shape[0] // 2
     owner_col = jnp.broadcast_to(own[...], (W, W)).astype(F32)
@@ -276,15 +405,23 @@
     for d in range(1, NR):
         arrived(inv_cols.at[lanes(z), :], inv_s.at[d - 1])
     for c, rows in enumerate(chunks):
-        sent(gath, rows, g1_s.at[c])
-        for i in range(NP // 2):
+        piece = by_lanes(gath, rows)
+        sent_near(piece, g1_s.at[c])
+        sent_far(piece, g1_s.at[c])
+        for i in range(4, 8):
             arrived(mine.at[rows, :], st_s.at[c, i])
 
-    @pl.when(core == 0)
+        @pl.when(core == 0)
+        def _():
+            for i in range(4):
+                arrived(mine.at[rows, :], st_s.at[c, i])
+
+    @pl.when(folds)
     def _():
-        for c, rows in enumerate(chunks):
-            sent(solved.at[0], rows, ag_s.at[c])
-            arrived(solved.at[0].at[rows, :], fw_s.at[c])
+        sent_near(by_rows(low), low_s)
+        sent_far(by_rows(low), low_s)
+
+    sent_block(jnp.int32(NP - 1), True)
 
     @pl.loop(1, peers)
     def _(i):
@@ -300,8 +437,8 @@
     depth = factor.shape[3]
     span = NR * W
     rows = parent_in.shape[1]
-    first = (sources // 2 + 15) // 16 * 16
-    chunks = (pl.ds(0, first), pl.ds(first, sources - first))
+    size = sources // 3
+    chunks = tuple(pl.ds(i * size, size) for i in range(3))
     ns = len(chunks)
     any_spec, vmem = pl.BlockSpec(memory_space=pl.ANY), pl.BlockSpec(memory_space=pltpu.VMEM)
     dma = pltpu.SemaphoreType.DMA
@@ -319,7 +456,9 @@
             pltpu.VMEM((2 * W, depth), BF16),
             pltpu.VMEM((span, W), F32),
             pltpu.VMEM((span, 2 * W), BF16),
+            pltpu.VMEM((span, span), F32),
             pltpu.VMEM((sources, span), F32),
+            pltpu.VMEM((sources, W), F32),
             pltpu.VMEM((NP, sources, span), F32),
             pltpu.VMEM((sources, W), F32),
             pltpu.VMEM((sources, 2 * W), F32),
@@ -328,15 +467,17 @@
             pltpu.VMEM((2 * W, rows), F32),
             pltpu.VMEM((max(1, fronts - 1), 2 * W // fronts, rows), F32),
             pltpu.VMEM((2 * W, rows), F32),
-            dma((3,)),
+            dma((4,)),
             dma((NR - 1,)),
             dma((NR - 1,)),
+            dma((8,)),
+            dma((8,)),
             dma((ns, 8)),
             dma((ns, 8)),
-            dma((ns, NP // 2)),
             dma((ns, 8)),
+            dma((2, ns, 8)),
             dma((NP, ns, 9)),
-            dma((ns,)),
+            dma((2, ns)),
             dma((NP, ns)),
             dma((NP * NR,)),
             dma((NP * NR,)),

time: 225 us -> 194 us (0.86)
  Pallas kernels: 220 us -> 188 us
    pallas_call x1, Pallas kernels: 220 us -> 188 us  [shards(): pl.pallas_call(functools.partial(kernel, chunks, fronts), out_shape=(jax....]
where the time goes in v2:
time: 194 us; the launch traced here: 193 us
  Pallas kernels  188 us (97%)
  local copies, waits for them, and re-layouts  4.6 us (2%)
    pallas_call x1, Pallas kernels, shards(): pl.pallas_call(functools.partial(kernel, chunks, fronts), out_shape=(jax....  188 us

profile of v2, /device:TPU:1, one launch (start us, length us, event | category | flops | bytes accessed | tf_op | source)
XLA Modules:
  0.0 193.4 jit_solution(9355129305055937339)
XLA Ops:
  0.6 1.4 copy.10.own
  2.0 188.2 %shard_map.95 = (f32[240,128]{1,0:T(8,128)}, f32[240,256]{1,0:T(8,128)}) custom-call(f32[128,8192]{1,0:T(8,128)} %bitcast.7, f32[128,8192]{1,0:T(8,128)} %bitcast.8, f32[128,1024]{1,0:T(8,128)} %bitcast.9, f32[240,128]{1,0:T(8,128)} %bitcast.10, f32[240,128]{1,0:T(8,128)} %bitcast.11, s32[128,1]{1,0:T(8,128)} %copy.10.own, s32[1,128]{1,0:T(1,128)} %slot.1, ...), custom_call_target="tpu_custom_call" | custom-call | tf_op jit(solution)/shard_map/pallas_call | solution.py:445
  190.2 1.6 copy.13
  191.8 1.7 copy.14

commit v3 on v2

--- a/solution.py
+++ b/solution.py
@@ -31,7 +31,7 @@
 
 def kernel(
     chunks, fronts, fac, bnd, inv, rhs, brhs, own, slot, par, out_sol, out_par,
-    stage, wh, wl, inv_cols, inv_hl, low, gath, based, solved, mine, acc, tosend, got, part, quarters, summed,
+    stage, wh, wl, inv_cols, inv_hl, low, gath, based, solved, mine, acc, pick, tosend, got, part, quarters, summed,
     load_sem, inv_s, inv_r, low_s, low_r, g1_s, g1_r, st_s, ag_s, ag_r, fw_s, fw_r, own_s, own_r,
     rs_s, rs_r, fa_s, fa_r,
 ):
@@ -139,8 +139,9 @@
     def gathered(c, rows):
         finish(by_lanes(gath, rows), g1_r.at[c])
         hi, lo = halves(gath[rows, :])
-        both = mul(hi, inv_hl[...], NN)
-        return both[:, :W] + both[:, W:] + mul(lo, inv_hl[:, pl.ds(0, W)], NN)
+        both = mul(jnp.concatenate([hi, lo], axis=0), inv_hl[...], NN)
+        both = both[:, :W] + both[:, W:]
+        return both[:rows.size] + both[rows.size:]
 
     def send_solved(k, c, rows):
         target = lax.rem(k + 1, NP)
@@ -216,6 +217,18 @@
     @pl.when(core == 1)
     def _():
         send_inv()
+
+    owner_row = jnp.broadcast_to(own[...], (W, W)).astype(F32)
+    owner_col = owner_row.T
+    first = lax.broadcasted_iota(jnp.int32, (W, W), 0)
+    second = lax.broadcasted_iota(jnp.int32, (W, W), 1)
+    earlier = jnp.where((owner_col == owner_row) & (first < second), 1.0, 0.0)
+    position = jnp.sum(earlier, axis=0, keepdims=True)
+    tile = owner_row[0:1, :] * (2 * CAP) + position
+    row_id = lax.broadcasted_iota(jnp.int32, (peers * 2 * CAP, W), 0).astype(F32)
+    pick[...] = jnp.concatenate(
+        [jnp.where(row_id == tile, 1.0, 0.0), jnp.where(row_id == tile + CAP, 1.0, 0.0)], axis=1
+    ).astype(BF16)
 
     load_i.wait()
     for d in range(1, NR):
@@ -283,7 +296,8 @@
                 arrived(block.at[rows, :], fw_r.at[k, c])
 
             hi, lo = halves(block[rows, :])
-            term = mul(hi, wh[:, wide(k)], NT) + mul(lo, wh[:, wide(k)], NT) + mul(hi, wl[:, wide(k)], NT)
+            both = mul(jnp.concatenate([hi, lo], axis=0), wh[:, wide(k)], NT)
+            term = both[:rows.size] + both[rows.size:] + mul(hi, wl[:, wide(k)], NT)
 
             @pl.when((p == k + 1) & folds)
             def _():
@@ -322,17 +336,6 @@
         sent_block(k - 1, k > 0)
 
     half = mine.shape[0] // 2
-    owner_col = jnp.broadcast_to(own[...], (W, W)).astype(F32)
-    owner_row = owner_col.T
-    first = lax.broadcasted_iota(jnp.int32, (W, W), 0)
-    second = lax.broadcasted_iota(jnp.int32, (W, W), 1)
-    earlier = jnp.where((owner_col == owner_row) & (first < second), 1.0, 0.0)
-    position = jnp.sum(earlier, axis=0, keepdims=True)
-    tile = owner_row[0:1, :] * (2 * CAP) + position
-    row_id = lax.broadcasted_iota(jnp.int32, (peers * 2 * CAP, W), 0).astype(F32)
-    pick = jnp.concatenate(
-        [jnp.where(row_id == tile, 1.0, 0.0), jnp.where(row_id == tile + CAP, 1.0, 0.0)], axis=1
-    ).astype(BF16)
     update = brhs[...] - acc[:, pl.ds(W, W)]
     tail = jnp.where(
         lax.broadcasted_iota(jnp.int32, (W - half, W), 0) == 0,
@@ -347,7 +350,7 @@
         axis=1,
     )
     hi, lo = halves(ext)
-    tosend[...] = mul(pick, hi, NT) + mul(pick, lo, NT)
+    tosend[...] = mul(pick[...], hi, NT) + mul(pick[...], lo, NT)
 
     def tiles(i):
         return pl.ds(pl.multiple_of(i * 2 * CAP, 2 * CAP), 2 * CAP)
@@ -361,6 +364,27 @@
         ).start()
 
     got[tiles(me), :] = tosend[tiles(me), :]
+
+    for d in range(1, NR):
+        arrived(inv_cols.at[lanes(z), :], inv_s.at[d - 1])
+    for c, rows in enumerate(chunks):
+        piece = by_lanes(gath, rows)
+        sent_near(piece, g1_s.at[c])
+        sent_far(piece, g1_s.at[c])
+        for i in range(4, 8):
+            arrived(mine.at[rows, :], st_s.at[c, i])
+
+        @pl.when(core == 0)
+        def _():
+            for i in range(4):
+                arrived(mine.at[rows, :], st_s.at[c, i])
+
+    @pl.when(folds)
+    def _():
+        sent_near(by_rows(low), low_s)
+        sent_far(by_rows(low), low_s)
+
+    sent_block(jnp.int32(NP - 1), True)
 
     @pl.loop(1, peers)
     def _(i):
@@ -385,48 +409,26 @@
     for i in range(1, fronts):
         t = lax.rem(f + i, fronts)
         remote(part.at[bands(t), :], quarters.at[i - 1], rs_s.at[i - 1], rs_r.at[i - 1], (t, p, z)).start()
+    @pl.loop(1, peers)
+    def _(i):
+        arrived(tosend.at[tiles(0), :], own_s.at[i])
+
     for i in range(1, fronts):
         arrived(quarters.at[i - 1], rs_r.at[i - 1])
     total = part[bands(f), :]
     for i in range(1, fronts):
         total = total + quarters[i - 1]
-    for i in range(1, fronts):
-        arrived(quarters.at[i - 1], rs_s.at[i - 1])
     summed[bands(f), :] = total
     for i in range(1, fronts):
         t = lax.rem(f + i, fronts)
         remote(summed.at[bands(f), :], summed.at[bands(f), :], fa_s.at[i - 1], fa_r.at[i - 1], (t, p, z)).start()
+    out_sol[...] = mine[...]
+    for i in range(1, fronts):
+        arrived(quarters.at[i - 1], rs_s.at[i - 1])
     for i in range(1, fronts):
         arrived(summed.at[bands(lax.rem(f + fronts - i, fronts)), :], fa_r.at[i - 1])
     out_par[0:half, :] = par[0:half, :] + summed[0:half, :]
     out_par[half:2 * half, :] = par[half:2 * half, :] + summed[W:W + half, :]
-    out_sol[...] = mine[...]
-
-    for d in range(1, NR):
-        arrived(inv_cols.at[lanes(z), :], inv_s.at[d - 1])
-    for c, rows in enumerate(chunks):
-        piece = by_lanes(gath, rows)
-        sent_near(piece, g1_s.at[c])
-        sent_far(piece, g1_s.at[c])
-        for i in range(4, 8):
-            arrived(mine.at[rows, :], st_s.at[c, i])
-
-        @pl.when(core == 0)
-        def _():
-            for i in range(4):
-                arrived(mine.at[rows, :], st_s.at[c, i])
-
-    @pl.when(folds)
-    def _():
-        sent_near(by_rows(low), low_s)
-        sent_far(by_rows(low), low_s)
-
-    sent_block(jnp.int32(NP - 1), True)
-
-    @pl.loop(1, peers)
-    def _(i):
-        arrived(tosend.at[tiles(0), :], own_s.at[i])
-
     for i in range(1, fronts):
         arrived(part.at[bands(f), :], fa_s.at[i - 1])
 
@@ -437,8 +439,8 @@
     depth = factor.shape[3]
     span = NR * W
     rows = parent_in.shape[1]
-    size = sources // 3
-    chunks = tuple(pl.ds(i * size, size) for i in range(3))
+    size = (sources // 4 + 15) // 16 * 16
+    chunks = tuple(pl.ds(i, min(size, sources - i)) for i in range(0, sources, size))
     ns = len(chunks)
     any_spec, vmem = pl.BlockSpec(memory_space=pl.ANY), pl.BlockSpec(memory_space=pltpu.VMEM)
     dma = pltpu.SemaphoreType.DMA
@@ -462,6 +464,7 @@
             pltpu.VMEM((NP, sources, span), F32),
             pltpu.VMEM((sources, W), F32),
             pltpu.VMEM((sources, 2 * W), F32),
+            pltpu.VMEM((NP * NR * 2 * CAP, 2 * W), BF16),
             pltpu.VMEM((NP * NR * 2 * CAP, W), F32),
             pltpu.VMEM((NP * NR * 2 * CAP, W), F32),
             pltpu.VMEM((2 * W, rows), F32),
@@ -487,7 +490,7 @@
             dma((fronts,)),
         ],
         compiler_params=pltpu.CompilerParams(collective_id=0, has_side_effects=True, vmem_limit_bytes=60 << 20),
-    )(factor[0, 0], boundary[0], inv_diag[0, 0], rhs[0], boundary_rhs[0], owner[0], slot, parent_in)
+    )(factor[0, 0], boundary[0], inv_diag[0, 0], rhs[0], boundary_rhs[0], owner[:, :, 0], slot, parent_in)
 
 
 def body(*args):

time: 194 us -> 190 us (0.979)
  Pallas kernels: 188 us -> 186 us
    pallas_call x1, Pallas kernels: 188 us -> 186 us  [shards(): pl.pallas_call(functools.partial(kernel, chunks, fronts), out_shape=(jax....]
where the time goes in v3:
time: 190 us
  Pallas kernels  186 us (98%)
  local copies, waits for them, and re-layouts  3.21 us (2%)
    pallas_call x1, Pallas kernels, shards(): pl.pallas_call(functools.partial(kernel, chunks, fronts), out_shape=(jax....  186 us

profile of v3, /device:TPU:1, one launch (start us, length us, event | category | flops | bytes accessed | tf_op | source)
XLA Modules:
  0.0 189.5 jit_solution(13810927688884078493)
XLA Ops:
  0.6 185.7 %shard_map.95 = (f32[240,128]{1,0:T(8,128)}, f32[240,256]{1,0:T(8,128)}) custom-call(f32[128,8192]{1,0:T(8,128)} %bitcast.7, f32[128,8192]{1,0:T(8,128)} %bitcast.8, f32[128,1024]{1,0:T(8,128)} %bitcast.9, f32[240,128]{1,0:T(8,128)} %bitcast.10, f32[240,128]{1,0:T(8,128)} %bitcast.11, s32[1,128]{1,0:T(1,128)} %bitcast.13, s32[1,128]{1,0:T(1,128)} %slot.1, ...), custom_call_target="tpu_custom_call" | custom-call | tf_op jit(solution)/shard_map/pallas_call | solution.py:447
  186.3 1.6 copy.12
  187.9 1.7 copy.13

commit v4 on v3

--- a/solution.py
+++ b/solution.py
@@ -13,7 +13,7 @@
 NN = (((1,), (0,)), ((), ()))
 NP, NR, W = 8, 8, 128
 CAP = 4
-FOLDS = {4: (-1, 1, 1), 6: (-1, 1, 3)}
+FOLDS = {4: (-1, 1, 1), 6: (-1, 1, 2)}
 
 
 def halves(x):
@@ -440,7 +440,8 @@
     span = NR * W
     rows = parent_in.shape[1]
     size = (sources // 4 + 15) // 16 * 16
-    chunks = tuple(pl.ds(i, min(size, sources - i)) for i in range(0, sources, size))
+    cuts = [0, *range(sources - (sources - 1) // size * size, sources + 1, size)]
+    chunks = tuple(pl.ds(i, j - i) for i, j in zip(cuts, cuts[1:]))
     ns = len(chunks)
     any_spec, vmem = pl.BlockSpec(memory_space=pl.ANY), pl.BlockSpec(memory_space=pltpu.VMEM)
     dma = pltpu.SemaphoreType.DMA

time: 190 us -> 189 us (level)
  Pallas kernels: 186 us -> 184 us
where the time goes in v4:
time: 189 us; the launch traced here: 188 us
  Pallas kernels  184 us (97%)
  local copies, waits for them, and re-layouts  3.21 us (2%)
    pallas_call x1, Pallas kernels, shards(): pl.pallas_call(functools.partial(kernel, chunks, fronts), out_shape=(jax....  184 us

profile of v4, /device:TPU:1, one launch (start us, length us, event | category | flops | bytes accessed | tf_op | source)
XLA Modules:
  0.0 188.2 jit_solution(15183772819678452308)
XLA Ops:
  0.6 184.4 %shard_map.95 = (f32[240,128]{1,0:T(8,128)}, f32[240,256]{1,0:T(8,128)}) custom-call(f32[128,8192]{1,0:T(8,128)} %bitcast.7, f32[128,8192]{1,0:T(8,128)} %bitcast.8, f32[128,1024]{1,0:T(8,128)} %bitcast.9, f32[240,128]{1,0:T(8,128)} %bitcast.10, f32[240,128]{1,0:T(8,128)} %bitcast.11, s32[1,128]{1,0:T(1,128)} %bitcast.13, s32[1,128]{1,0:T(1,128)} %slot.1, ...), custom_call_target="tpu_custom_call" | custom-call | tf_op jit(solution)/shard_map/pallas_call | solution.py:448
  185.0 1.6 copy.12
  186.6 1.7 copy.13
